TPU v7x, 32 devices: a whole 2x2x4 slice. The times are simulated.
32 devices in a mesh: tensor: 2 (over y), context: 16 (over z, x, core).
Axes of the slice: x: 2, y: 2, z: 4, core: 2. Of those that a mesh axis runs over, the one named last changes fastest.
Arguments:
- query_stream: bfloat16 [8192, 2048], P('tensor', 'context'), may hold values from -6 to 6
- key_stream: bfloat16 [8192, 2048], P('tensor', 'context'), may hold values from -6 to 6
- value_stream: bfloat16 [8192, 2048], P('tensor', 'context'), may hold values from -6 to 6
- filter_taps: bfloat16 [2048, 8192], P(('tensor', 'context')), may hold values from -0.125 to 0.125
- short_filters: float32 [3, 3, 8192], P(None, None, ('tensor', 'context')), may hold values from -3 to 3
- skip_gain: float32 [8192], P(('tensor', 'context')), may hold values from 0.5 to 1.5
Outputs:
- gated_out: bfloat16 [8192, 2048], P('tensor', 'context')
All inputs are finite; a program needn't handle non-finite values.
Results may differ from a plain program's by a relative error of at most 0.0057.
Values may be sent and summed in bfloat16 or wider, within the bound.
A program may use at most 128 MiB of HBM per device.

v0:
```python
import functools

import jax
import jax.numpy as jnp
import ml_dtypes
import numpy as np
from jax import lax
from jax.experimental import pallas as pl
from jax.experimental.pallas import tpu as pltpu
from jax.sharding import PartitionSpec as P

F32, BF16 = jnp.float32, jnp.bfloat16
MESH = pl.DeviceIdType.MESH


def split(table):
    high = table.astype(ml_dtypes.bfloat16)
    low = (table - high.astype(np.float64)).astype(ml_dtypes.bfloat16)
    return jnp.asarray(high), jnp.asarray(low)


def tables(block):
    n = np.arange(2 * block)
    f = np.arange(block)
    phase = (n[:, None] * (2 * f[None, :] + 1)) % (4 * block)
    angle = phase * (2.0 * np.pi / (4 * block))
    forward = np.concatenate([np.cos(angle), -np.sin(angle)], axis=1)
    inverse = forward[block:].T / block
    return split(forward), split(inverse)


def params(**kw):
    return pltpu.CompilerParams(vmem_limit_bytes=60 * 1024 * 1024, **kw)


def columns(weights, rim):
    rest = jnp.zeros((128 - weights.shape[0] - rim.shape[0], weights.shape[1]), F32)
    return jnp.concatenate([weights, rim, rest], axis=0).T


def short_filter(signal, table, stream):
    signal = signal.astype(F32)
    at = lambda k: table[:, k : k + 1]
    lane = lax.broadcasted_iota(jnp.int32, signal.shape, 1)
    before2, before1 = at(16 + 2 * stream), at(17 + 2 * stream)
    lag1 = jnp.where(lane == 0, before1, pltpu.roll(signal, 1, 1))
    lag2 = jnp.where(lane == 0, before2, jnp.where(lane == 1, before1, pltpu.roll(signal, 2, 1)))
    return at(3 * stream) * signal + at(3 * stream + 1) * lag1 + at(3 * stream + 2) * lag2


def greet(count, devices):
    barrier = pltpu.get_barrier_semaphore()

    @pl.loop(1, count)
    def _(step):
        pl.semaphore_signal(barrier, inc=1, device_id=devices(step), device_id_type=MESH)

    pl.semaphore_wait(barrier, count - 1)


def settle(ref, sem):
    pltpu.make_async_copy(ref, ref, sem).wait()


def send(source, target, send_sem, recv_sem, device):
    pltpu.make_async_remote_copy(
        src_ref=source, dst_ref=target, send_sem=send_sem, recv_sem=recv_sem, device_id=device, device_id_type=MESH
    ).start()


def exchange_kernel(
    context_size, tensor_size,
    q_ref, k_ref, v_ref, own_ref, taps_ref, high_ref, low_ref,
    x_ref, spectra_ref, query_ref,
    weights_ref, edge_ref, rim_ref, products_ref, h_ref, send_sem, recv_sem,
):
    me = lax.axis_index("context")
    everyone = context_size * tensor_size
    whoami = lax.axis_index("tensor") * context_size + me
    chans = products_ref.shape[1]
    width = q_ref.shape[1]
    peer = lambda step: lax.rem(me + step, context_size)
    anyone = lambda step: lax.rem(whoami + step, everyone)
    address = lambda d: {"tensor": lax.div(d, context_size), "context": lax.rem(d, context_size)}
    greet(everyone, lambda step: address(anyone(step)))

    @pl.loop(1, context_size)
    def _(step):
        send(own_ref, weights_ref.at[me], send_sem.at[0], recv_sem.at[0], {"context": peer(step)})

    pltpu.make_async_copy(own_ref, weights_ref.at[me], recv_sem.at[0]).start()

    row = lax.broadcasted_iota(jnp.int32, (8, width), 0)
    col = lax.broadcasted_iota(jnp.int32, (8, width), 1)

    @pl.loop(0, context_size)
    def _(group):
        rows = pl.ds(pl.multiple_of(group * chans, chans), chans)
        total = jnp.zeros((8, chans), F32)
        for stream, ref in enumerate((q_ref, k_ref, v_ref)):
            pick = jnp.where(
                (row >= 2 * stream) & (row < 2 * stream + 2) & (col == width - 2 + row - 2 * stream), 1.0, 0.0
            ).astype(BF16)
            total = total + lax.dot_general(
                pick, ref[rows, :], (((1,), (1,)), ((), ())), preferred_element_type=F32
            )
        edge_ref[group] = total.astype(BF16)

    send(edge_ref, rim_ref, send_sem.at[1], recv_sem.at[1], {"context": peer(1)})

    def piece(d):
        if taps_ref.ndim == 3:
            return taps_ref.at[d]
        return taps_ref.at[:, pl.ds(pl.multiple_of(d * chans, chans), chans)]

    @pl.loop(1, everyone)
    def _(step):
        d = anyone(step)
        send(piece(d), h_ref.at[whoami], send_sem.at[2], recv_sem.at[2], address(d))

    pltpu.make_async_copy(piece(whoami), h_ref.at[whoami], recv_sem.at[2]).start()

    settle(weights_ref, recv_sem.at[0])
    settle(rim_ref, recv_sem.at[1])
    kept = jnp.where(me == 0, 0.0, 1.0).astype(F32)

    def table_of(group):
        return columns(weights_ref[group], rim_ref[group].astype(F32) * kept)

    @pl.loop(1, context_size + 1)
    def _(step):
        group = peer(step)
        rows = pl.ds(pl.multiple_of(group * chans, chans), chans)
        table = table_of(group)
        products_ref[group] = (
            short_filter(k_ref[rows, :], table, 1) * short_filter(v_ref[rows, :], table, 2)
        ).astype(BF16)

        @pl.when(step < context_size)
        def _():
            send(products_ref.at[group], x_ref.at[me], send_sem.at[3], recv_sem.at[3], {"context": group})

        @pl.when(step == context_size)
        def _():
            pltpu.make_async_copy(products_ref.at[group], x_ref.at[me], recv_sem.at[3]).start()

    @pl.loop(0, context_size)
    def _(group):
        rows = pl.ds(pl.multiple_of(group * chans, chans), chans)
        query_ref[rows, :] = short_filter(q_ref[rows, :], table_of(group), 0)

    settle(h_ref, recv_sem.at[2])
    blocks, block = spectra_ref.shape[0], spectra_ref.shape[2] // 2
    slabs = block // h_ref.shape[1]
    dims = (((0,), (0,)), ((), ()))

    @pl.loop(0, blocks)
    def _(index):
        h = jnp.concatenate([h_ref[index * slabs + part] for part in range(slabs)], axis=0)
        spectra_ref[index] = lax.dot_general(
            h, high_ref[:block], dims, preferred_element_type=F32
        ) + lax.dot_general(h, low_ref[:block], dims, preferred_element_type=F32)

    settle(weights_ref.at[pl.ds(0, context_size - 1)], send_sem.at[0])
    settle(edge_ref, send_sem.at[1])
    settle(h_ref.at[pl.ds(0, everyone - 1)], send_sem.at[2])
    settle(products_ref.at[pl.ds(0, context_size - 1)], send_sem.at[3])
    settle(x_ref, recv_sem.at[3])


def conv_kernel(
    step, x_ref, h_ref, skip_ref, high_ref, low_ref, back_high_ref, back_low_ref,
    out_ref, spec_ref, mixed_ref, sent_ref, send_sem, recv_sem,
):
    me = lax.axis_index("context")
    pieces = x_ref.shape[0]
    peer = lambda k: lax.rem(me + k, pieces)
    greet(pieces, lambda k: {"context": peer(k)})

    @pl.loop(0, x_ref.shape[1] // step)
    def _(chunk):
        rows = pl.ds(pl.multiple_of(chunk * step, step), step)
        conv_chunk(
            x_ref.at[:, rows], h_ref.at[:, rows], skip_ref.at[rows], high_ref, low_ref, back_high_ref, back_low_ref,
            sent_ref.at[:, rows], spec_ref, mixed_ref,
        )

        @pl.loop(1, pieces)
        def _(k):
            send(sent_ref.at[peer(k), rows], out_ref.at[me, rows], send_sem, recv_sem, {"context": peer(k)})

        pltpu.make_async_copy(sent_ref.at[me, rows], out_ref.at[me, rows], recv_sem).start()

    settle(sent_ref.at[pl.ds(0, pieces - 1)], send_sem)
    settle(out_ref, recv_sem)


def conv_chunk(x_ref, h_ref, skip_ref, high_ref, low_ref, back_high_ref, back_low_ref, out_ref, spec_ref, mixed_ref):
    pieces, chans, width = x_ref.shape
    blocks = pieces // 2
    half = 2 * width
    zero = jnp.zeros((chans, width), BF16)
    piece = lambda p: zero if p < 0 else x_ref[p]
    parts = [jnp.concatenate([piece(2 * j - 2 + lag) for j in range(blocks)], axis=0) for lag in range(4)]
    stacked = jnp.concatenate(parts, axis=1)
    spec_ref[...] = jnp.dot(stacked, high_ref[...], preferred_element_type=F32) + jnp.dot(
        stacked, low_ref[...], preferred_element_type=F32
    )

    @pl.loop(0, chans // 8)
    def _(group):
        base = pl.multiple_of(group * 8, 8)
        for lanes in range(half // 128):
            real, imag = pl.ds(lanes * 128, 128), pl.ds(half + lanes * 128, 128)
            rows = [pl.ds(pl.multiple_of(j * chans + base, 8), 8) for j in range(blocks)]
            xr = [spec_ref[r, real] for r in rows]
            xi = [spec_ref[r, imag] for r in rows]
            hr = [h_ref[j, pl.ds(base, 8), real] for j in range(blocks)]
            hi = [h_ref[j, pl.ds(base, 8), imag] for j in range(blocks)]
            for i in range(blocks):
                yr = xr[i] * hr[0] - xi[i] * hi[0]
                yi = xr[i] * hi[0] + xi[i] * hr[0]
                for j in range(i):
                    d = i - j
                    yr = yr + xr[j] * hr[d] - xi[j] * hi[d]
                    yi = yi + xr[j] * hi[d] + xi[j] * hr[d]
                mixed_ref[rows[i], real] = yr
                mixed_ref[rows[i], imag] = yi

    spectrum = mixed_ref[...]
    top = spectrum.astype(BF16)
    rest = (spectrum - top.astype(F32)).astype(BF16)
    conv = (
        jnp.dot(top, back_high_ref[...], preferred_element_type=F32)
        + jnp.dot(rest, back_high_ref[...], preferred_element_type=F32)
        + jnp.dot(top, back_low_ref[...], preferred_element_type=F32)
    )
    skip = skip_ref[...]
    for j in range(blocks):
        for side in range(2):
            part = conv[j * chans : (j + 1) * chans, side * width : (side + 1) * width]
            out_ref[2 * j + side] = (part + skip * x_ref[2 * j + side].astype(F32)).astype(BF16)


def local(query_stream, key_stream, value_stream, filter_taps, short_filters, skip_gain):
    group_width, block_rows = query_stream.shape
    context_size = lax.axis_size("context")
    tensor_size = lax.axis_size("tensor")
    everyone = tensor_size * context_size
    chans = group_width // context_size
    offset_rows = filter_taps.shape[0]
    block = 2 * block_rows
    blocks = context_size // 2
    (high, low), (back_high, back_low) = tables(block)

    vmem = pl.BlockSpec(memory_space=pltpu.VMEM)
    weights = jnp.pad(short_filters.reshape(9, chans), ((0, 7), (0, 0)))
    taps = filter_taps
    if chans % 128:
        taps = taps.reshape(offset_rows, everyone, chans).transpose(1, 0, 2)
    pieces = (context_size, chans, block_rows)
    dma = pltpu.SemaphoreType.DMA
    arrived, spectra, query_short = pl.pallas_call(
        functools.partial(exchange_kernel, context_size, tensor_size),
        in_specs=[vmem] * 4 + [pl.BlockSpec(memory_space=pl.ANY)] + [vmem] * 2,
        out_specs=[vmem] * 3,
        out_shape=[
            jax.ShapeDtypeStruct(pieces, BF16),
            jax.ShapeDtypeStruct((blocks, chans, 2 * block), F32),
            jax.ShapeDtypeStruct((group_width, block_rows), F32),
        ],
        scratch_shapes=[
            pltpu.VMEM((context_size, 16, chans), F32),
            pltpu.VMEM((context_size, 8, chans), BF16),
            pltpu.VMEM((context_size, 8, chans), BF16),
            pltpu.VMEM(pieces, BF16),
            pltpu.VMEM((everyone, offset_rows, chans), BF16),
            dma((4,)),
            dma((4,)),
        ],
        compiler_params=params(collective_id=0, has_side_effects=True),
    )(query_stream, key_stream, value_stream, weights, taps, high, low)

    step = min(chans, 64)
    returned = pl.pallas_call(
        functools.partial(conv_kernel, step),
        in_specs=[vmem] * 7,
        out_specs=vmem,
        out_shape=jax.ShapeDtypeStruct(pieces, BF16),
        scratch_shapes=[pltpu.VMEM((blocks * step, 2 * block), F32)] * 2
        + [pltpu.VMEM(pieces, BF16), dma, dma],
        compiler_params=params(collective_id=1, has_side_effects=True),
    )(arrived, spectra, skip_gain[:, None], high, low, back_high, back_low)
    return (query_short * returned.reshape(group_width, block_rows).astype(F32)).astype(BF16)


def solution(mesh):
    placed = (
        P("tensor", "context"),
        P("tensor", "context"),
        P("tensor", "context"),
        P(("tensor", "context"), None),
        P(None, None, ("tensor", "context")),
        P(("tensor", "context")),
    )
    return jax.shard_map(
        local, mesh=mesh, in_specs=placed, out_specs=P("tensor", "context"), check_vma=False
    )
```

profile of v0, /device:TPU:0, one launch (start us, length us, event | category | flops | bytes accessed | tf_op | source)
XLA Modules:
  0.0 100.7 jit_solution(10307517235770750717)
XLA Ops:
  0.0 0.7 reshape.6
  0.7 0.6 pad.4.own_ref
  1.3 1.5 %copy.11.skip_ref = f32[256,1]{1,0:T(8,128)} copy(f32[256,1]{0,1:T(1,128)} %bitcast.4) | data formatting | bytes 2048 | tf_op jit(solution)/shard_map/broadcast_in_dim | solution.py:293
  2.8 55.2 %shard_map.100 = (bf16[16,256,128]{2,1,0:T(8,128)(2,1)}, f32[8,256,512]{2,1,0:T(8,128)}, f32[4096,128]{1,0:T(8,128)}) custom-call(bf16[4096,128]{1,0:T(8,128)(2,1)} %q_ref.1, bf16[4096,128]{1,0:T(8,128)(2,1)} %k_ref.1, bf16[4096,128]{1,0:T(8,128)(2,1)} %v_ref.1, f32[16,256]{1,0:T(8,128)} %pad.4.own_ref, bf16[64,8192]{1,0:T(8,128)(2,1)} %taps_ref.1, ...), custom_call_target="tpu_custom_call" | custom-call | tf_op jit(solution)/shard_map/pallas_call | solution.py:263
  58.0 0.0 copy-start
  58.0 40.3 %shard_map.101 = bf16[16,256,128]{2,1,0:T(8,128)(2,1)} custom-call(bf16[16,256,128]{2,1,0:T(8,128)(2,1)} %get-tuple-element.9.x_ref, f32[8,256,512]{2,1,0:T(8,128)} %get-tuple-element.10.h_ref, f32[256,1]{1,0:T(8,128)} %copy.11.skip_ref, bf16[512,512]{1,0:T(8,128)(2,1)} %constant.11.clone.high_ref, bf16[512,512]{1,0:T(8,128)(2,1)} %constant.12.clone.low_ref, ...), custom_call_target="tpu_custom_call" | custom-call | tf_op jit(solution)/shard_map/pallas_call | solution.py:285
  98.3 0.0 copy-done
  98.3 2.4 %fusion = bf16[4096,128]{1,0:T(8,128)(2,1)} fusion(f32[4096,128]{1,0:T(8,128)S(1)} %copy-done, bf16[16,256,128]{2,1,0:T(8,128)(2,1)} %shard_map.101), kind=kLoop, calls=%fused_computation.1 | loop fusion | flops 1572864 | bytes 4194304 | tf_op jit(solution)/shard_map/convert_element_type | solution.py:294
Async XLA Ops:
  58.0 40.3 %copy-start = (f32[4096,128]{1,0:T(8,128)S(1)}, f32[4096,128]{1,0:T(8,128)}, u32[]{:S(2)}) copy-start(f32[4096,128]{1,0:T(8,128)} %get-tuple-element.8) | copy-start | bytes 6291460
where the time goes:
time: 101 us
  Pallas kernels  95.5 us (95%)
  local copies, waits for them, and re-layouts  2.79 us (3%)
  other arithmetic  2.4 us (2%)
    pallas_call x1, Pallas kernels, local(): pl.pallas_call(functools.partial(exchange_kernel, context_size, tensor_si...  55.2 us
    pallas_call x1, Pallas kernels, local(): pl.pallas_call(functools.partial(conv_kernel, step), in_specs=[vmem] * 7,...  40.3 us
    convert_element_type x1, other arithmetic, local(): (query_short * returned.reshape(group_width, block_rows).astype(F32)).ast...  2.4 us

commit v1 on v0

--- a/solution.py
+++ b/solution.py
@@ -68,11 +68,12 @@
     ).start()
 
 
-def exchange_kernel(
-    context_size, tensor_size,
-    q_ref, k_ref, v_ref, own_ref, taps_ref, high_ref, low_ref,
-    x_ref, spectra_ref, query_ref,
-    weights_ref, edge_ref, rim_ref, products_ref, h_ref, send_sem, recv_sem,
+def operator_kernel(
+    context_size, tensor_size, depth,
+    q_ref, k_ref, v_ref, short_ref, skip_ref, taps_ref, high_ref, low_ref, back_high_ref, back_low_ref,
+    out_ref,
+    own_ref, weights_ref, edge_ref, rim_ref, products_ref, h_ref, x_ref, spectra_ref, query_ref, gain_ref,
+    spec_ref, mixed_ref, sent_ref, back_ref, send_sem, recv_sem, chunk_sem, back_sem,
 ):
     me = lax.axis_index("context")
     everyone = context_size * tensor_size
@@ -83,6 +84,11 @@
     anyone = lambda step: lax.rem(whoami + step, everyone)
     address = lambda d: {"tensor": lax.div(d, context_size), "context": lax.rem(d, context_size)}
     greet(everyone, lambda step: address(anyone(step)))
+
+    own_ref[...] = jnp.zeros_like(own_ref)
+    for stream in range(3):
+        for lag in range(3):
+            own_ref[3 * stream + lag] = short_ref[stream, lag]
 
     @pl.loop(1, context_size)
     def _(step):
@@ -136,13 +142,24 @@
             short_filter(k_ref[rows, :], table, 1) * short_filter(v_ref[rows, :], table, 2)
         ).astype(BF16)
 
-        @pl.when(step < context_size)
-        def _():
-            send(products_ref.at[group], x_ref.at[me], send_sem.at[3], recv_sem.at[3], {"context": group})
-
-        @pl.when(step == context_size)
-        def _():
-            pltpu.make_async_copy(products_ref.at[group], x_ref.at[me], recv_sem.at[3]).start()
+    chunks = chans // depth
+    chunk_rows = lambda chunk: pl.ds(pl.multiple_of(chunk * depth, depth), depth)
+
+    @pl.loop(0, chunks)
+    def _(chunk):
+        rows = chunk_rows(chunk)
+
+        @pl.loop(1, context_size)
+        def _(step):
+            group = peer(step)
+            send(
+                products_ref.at[group, rows], x_ref.at[me, rows], send_sem.at[3], chunk_sem.at[chunk], {"context": group}
+            )
+
+        pltpu.make_async_copy(products_ref.at[me, rows], x_ref.at[me, rows], chunk_sem.at[chunk]).start()
+
+    gain = jnp.concatenate([skip_ref[...], jnp.zeros((127, chans), F32)], axis=0)
+    gain_ref[...] = gain.T
 
     @pl.loop(0, context_size)
     def _(group):
@@ -161,38 +178,37 @@
             h, high_ref[:block], dims, preferred_element_type=F32
         ) + lax.dot_general(h, low_ref[:block], dims, preferred_element_type=F32)
 
+    @pl.loop(0, chunks)
+    def _(chunk):
+        rows = chunk_rows(chunk)
+        settle(x_ref.at[:, rows], chunk_sem.at[chunk])
+        conv_chunk(
+            x_ref.at[:, rows], spectra_ref.at[:, rows], gain_ref.at[rows], high_ref, low_ref, back_high_ref,
+            back_low_ref, sent_ref.at[:, rows], spec_ref, mixed_ref,
+        )
+
+        @pl.loop(1, context_size)
+        def _(step):
+            group = peer(step)
+            send(sent_ref.at[group, rows], back_ref.at[me, rows], send_sem.at[4], back_sem.at[chunk], {"context": group})
+
+        pltpu.make_async_copy(sent_ref.at[me, rows], back_ref.at[me, rows], back_sem.at[chunk]).start()
+
+    @pl.loop(0, chunks)
+    def _(chunk):
+        rows = chunk_rows(chunk)
+        settle(back_ref.at[:, rows], back_sem.at[chunk])
+
+        @pl.loop(0, context_size)
+        def _(group):
+            flat = pl.ds(pl.multiple_of(group * chans + chunk * depth, depth), depth)
+            out_ref[flat, :] = (query_ref[flat, :] * back_ref[group, rows].astype(F32)).astype(BF16)
+
     settle(weights_ref.at[pl.ds(0, context_size - 1)], send_sem.at[0])
     settle(edge_ref, send_sem.at[1])
     settle(h_ref.at[pl.ds(0, everyone - 1)], send_sem.at[2])
     settle(products_ref.at[pl.ds(0, context_size - 1)], send_sem.at[3])
-    settle(x_ref, recv_sem.at[3])
-
-
-def conv_kernel(
-    step, x_ref, h_ref, skip_ref, high_ref, low_ref, back_high_ref, back_low_ref,
-    out_ref, spec_ref, mixed_ref, sent_ref, send_sem, recv_sem,
-):
-    me = lax.axis_index("context")
-    pieces = x_ref.shape[0]
-    peer = lambda k: lax.rem(me + k, pieces)
-    greet(pieces, lambda k: {"context": peer(k)})
-
-    @pl.loop(0, x_ref.shape[1] // step)
-    def _(chunk):
-        rows = pl.ds(pl.multiple_of(chunk * step, step), step)
-        conv_chunk(
-            x_ref.at[:, rows], h_ref.at[:, rows], skip_ref.at[rows], high_ref, low_ref, back_high_ref, back_low_ref,
-            sent_ref.at[:, rows], spec_ref, mixed_ref,
-        )
-
-        @pl.loop(1, pieces)
-        def _(k):
-            send(sent_ref.at[peer(k), rows], out_ref.at[me, rows], send_sem, recv_sem, {"context": peer(k)})
-
-        pltpu.make_async_copy(sent_ref.at[me, rows], out_ref.at[me, rows], recv_sem).start()
-
-    settle(sent_ref.at[pl.ds(0, pieces - 1)], send_sem)
-    settle(out_ref, recv_sem)
+    settle(sent_ref.at[pl.ds(0, context_size - 1)], send_sem.at[4])
 
 
 def conv_chunk(x_ref, h_ref, skip_ref, high_ref, low_ref, back_high_ref, back_low_ref, out_ref, spec_ref, mixed_ref):
@@ -235,7 +251,7 @@
         + jnp.dot(rest, back_high_ref[...], preferred_element_type=F32)
         + jnp.dot(top, back_low_ref[...], preferred_element_type=F32)
     )
-    skip = skip_ref[...]
+    skip = skip_ref[:, :1]
     for j in range(blocks):
         for side in range(2):
             part = conv[j * chans : (j + 1) * chans, side * width : (side + 1) * width]
@@ -254,44 +270,43 @@
     (high, low), (back_high, back_low) = tables(block)
 
     vmem = pl.BlockSpec(memory_space=pltpu.VMEM)
-    weights = jnp.pad(short_filters.reshape(9, chans), ((0, 7), (0, 0)))
     taps = filter_taps
     if chans % 128:
         taps = taps.reshape(offset_rows, everyone, chans).transpose(1, 0, 2)
-    pieces = (context_size, chans, block_rows)
+    depth = min(chans, 64)
+    chunks = chans // depth
+    pieces = pltpu.VMEM((context_size, chans, block_rows), BF16)
     dma = pltpu.SemaphoreType.DMA
-    arrived, spectra, query_short = pl.pallas_call(
-        functools.partial(exchange_kernel, context_size, tensor_size),
-        in_specs=[vmem] * 4 + [pl.BlockSpec(memory_space=pl.ANY)] + [vmem] * 2,
-        out_specs=[vmem] * 3,
-        out_shape=[
-            jax.ShapeDtypeStruct(pieces, BF16),
-            jax.ShapeDtypeStruct((blocks, chans, 2 * block), F32),
-            jax.ShapeDtypeStruct((group_width, block_rows), F32),
-        ],
+    return pl.pallas_call(
+        functools.partial(operator_kernel, context_size, tensor_size, depth),
+        in_specs=[vmem] * 5 + [pl.BlockSpec(memory_space=pl.ANY)] + [vmem] * 4,
+        out_specs=vmem,
+        out_shape=jax.ShapeDtypeStruct((group_width, block_rows), BF16),
         scratch_shapes=[
+            pltpu.VMEM((16, chans), F32),
             pltpu.VMEM((context_size, 16, chans), F32),
             pltpu.VMEM((context_size, 8, chans), BF16),
             pltpu.VMEM((context_size, 8, chans), BF16),
-            pltpu.VMEM(pieces, BF16),
+            pieces,
             pltpu.VMEM((everyone, offset_rows, chans), BF16),
-            dma((4,)),
-            dma((4,)),
+            pieces,
+            pltpu.VMEM((blocks, chans, 2 * block), F32),
+            pltpu.VMEM((group_width, block_rows), F32),
+            pltpu.VMEM((chans, 128), F32),
+            pltpu.VMEM((blocks * depth, 2 * block), F32),
+            pltpu.VMEM((blocks * depth, 2 * block), F32),
+            pieces,
+            pieces,
+            dma((5,)),
+            dma((3,)),
+            dma((chunks,)),
+            dma((chunks,)),
         ],
         compiler_params=params(collective_id=0, has_side_effects=True),
-    )(query_stream, key_stream, value_stream, weights, taps, high, low)
-
-    step = min(chans, 64)
-    returned = pl.pallas_call(
-        functools.partial(conv_kernel, step),
-        in_specs=[vmem] * 7,
-        out_specs=vmem,
-        out_shape=jax.ShapeDtypeStruct(pieces, BF16),
-        scratch_shapes=[pltpu.VMEM((blocks * step, 2 * block), F32)] * 2
-        + [pltpu.VMEM(pieces, BF16), dma, dma],
-        compiler_params=params(collective_id=1, has_side_effects=True),
-    )(arrived, spectra, skip_gain[:, None], high, low, back_high, back_low)
-    return (query_short * returned.reshape(group_width, block_rows).astype(F32)).astype(BF16)
+    )(
+        query_stream, key_stream, value_stream, short_filters, skip_gain[None, :], taps,
+        high, low, back_high, back_low,
+    )
 
 
 def solution(mesh):

time: 101 us -> 86 us (0.85)
  Pallas kernels: 95.5 us -> 83.6 us
  other arithmetic: 2.4 us -> 0 us
    pallas_call x2 -> x1, Pallas kernels: 95.5 us -> 83.6 us  [local(): pl.pallas_call(functools.partial(operator_kernel, context_size, tensor_si...]
    convert_element_type x1 -> x0, other arithmetic: 2.4 us -> none  [local(): (query_short * returned.reshape(group_width, block_rows).astype(F32)).ast...]
    unnamed x2 -> x1, local copies, waits for them, and re-layouts: 0.01 us -> 2.26 us
    broadcast_in_dim x1 -> x0, local copies, waits for them, and re-layouts: 1.47 us -> none  [local(): skip_gain[:, None]]
where the time goes in v1:
time: 86 us; the launch traced here: 85.9 us
  Pallas kernels  83.6 us (97%)
  local copies, waits for them, and re-layouts  2.26 us (3%)
    pallas_call x1, Pallas kernels, local(): pl.pallas_call(functools.partial(operator_kernel, context_size, tensor_si...  83.6 us
    unnamed x1, local copies, waits for them, and re-layouts  2.26 us

profile of v1, /device:TPU:0, one launch (start us, length us, event | category | flops | bytes accessed | tf_op | source)
XLA Modules:
  0.0 85.9 jit_solution(11981231692994772911)
XLA Ops:
  0.0 83.6 %shard_map.100 = bf16[4096,128]{1,0:T(8,128)(2,1)} custom-call(bf16[4096,128]{1,0:T(8,128)(2,1)} %q_ref.1, bf16[4096,128]{1,0:T(8,128)(2,1)} %k_ref.1, bf16[4096,128]{1,0:T(8,128)(2,1)} %v_ref.1, f32[3,3,256]{2,1,0:T(4,128)} %short_ref.1, f32[1,256]{1,0:T(1,128)} %bitcast.1, bf16[64,8192]{1,0:T(8,128)(2,1)} %taps_ref.1, ...), custom_call_target="tpu_custom_call" | custom-call | tf_op jit(solution)/shard_map/pallas_call | solution.py:280
  83.6 2.3 %copy.12 = bf16[4096,128]{1,0:T(8,128)(2,1)} copy(bf16[4096,128]{1,0:T(8,128)(2,1)} %shard_map.100) | data formatting | bytes 2097152

commit v2 on v1

--- a/solution.py
+++ b/solution.py
@@ -219,9 +219,7 @@
     piece = lambda p: zero if p < 0 else x_ref[p]
     parts = [jnp.concatenate([piece(2 * j - 2 + lag) for j in range(blocks)], axis=0) for lag in range(4)]
     stacked = jnp.concatenate(parts, axis=1)
-    spec_ref[...] = jnp.dot(stacked, high_ref[...], preferred_element_type=F32) + jnp.dot(
-        stacked, low_ref[...], preferred_element_type=F32
-    )
+    spec_ref[...] = jnp.dot(stacked, high_ref[...], preferred_element_type=F32)
 
     @pl.loop(0, chans // 8)
     def _(group):

time: 86 us -> 86 us (level)
  no operation moved by 1% of the time
where the time goes in v2:
time: 86 us; the launch traced here: 85.8 us
  Pallas kernels  83.5 us (97%)
  local copies, waits for them, and re-layouts  2.26 us (3%)
    pallas_call x1, Pallas kernels, local(): pl.pallas_call(functools.partial(operator_kernel, context_size, tensor_si...  83.5 us
    unnamed x1, local copies, waits for them, and re-layouts  2.26 us

profile of v2, /device:TPU:0, one launch (start us, length us, event | category | flops | bytes accessed | tf_op | source)
XLA Modules:
  0.0 85.8 jit_solution(1849606982575327542)
XLA Ops:
  0.0 83.5 %shard_map.100 = bf16[4096,128]{1,0:T(8,128)(2,1)} custom-call(bf16[4096,128]{1,0:T(8,128)(2,1)} %q_ref.1, bf16[4096,128]{1,0:T(8,128)(2,1)} %k_ref.1, bf16[4096,128]{1,0:T(8,128)(2,1)} %v_ref.1, f32[3,3,256]{2,1,0:T(4,128)} %short_ref.1, f32[1,256]{1,0:T(1,128)} %bitcast.1, bf16[64,8192]{1,0:T(8,128)(2,1)} %taps_ref.1, ...), custom_call_target="tpu_custom_call" | custom-call | tf_op jit(solution)/shard_map/pallas_call | solution.py:278
  83.6 2.3 %copy.12 = bf16[4096,128]{1,0:T(8,128)(2,1)} copy(bf16[4096,128]{1,0:T(8,128)(2,1)} %shard_map.100) | data formatting | bytes 2097152
